TPU v7x, 512 devices: a whole 4x8x8 slice. The times are simulated.
512 devices in a mesh: pipe: 8 (over y_lo, core), tensor: 64 (over y_hi, x, z).
Axes of the slice: x: 4, y: 8 (y_hi: 2, y_lo: 4; y = y_hi * 4 + y_lo), z: 8, core: 2. Of those that a mesh axis runs over, the one named last changes fastest.
Arguments:
- output_gradient: bfloat16 [8, 64, 2, 64, 1024], P('pipe', 'tensor'), may hold values from -6 to 6
- forward_input: bfloat16 [8, 2, 512, 8192], P('pipe', None, None, 'tensor'), may hold values from -6 to 6
- saved_rank_outputs: bfloat16 [8, 2, 512, 64], P('pipe', None, 'tensor'), may hold values from -6 to 6
- projection_weight: bfloat16 [8, 64, 1024, 1024], P('pipe', 'tensor'), may hold values from -0.0625 to 0.0625
- adapter_down_maps: bfloat16 [8, 8, 64, 8192], P('pipe', None, None, 'tensor'), may hold values from -0.75 to 0.75
- adapter_up_maps: bfloat16 [8, 64, 8, 8, 1024], P('pipe', 'tensor'), may hold values from -0.0625 to 0.0625
- segment_adapter_class: int32 [8, 2, 4], P('pipe'), may hold values from 0 to 7
- live_segment_table: int32 [8, 2], P('pipe'), may hold values from 1 to 4, as said below
Outputs:
- grad_prev: bfloat16 [8, 2, 512, 8192], P('pipe', None, None, 'tensor')
- down_map_gradient: bfloat16 [8, 8, 64, 8192], P('pipe', None, None, 'tensor')
- up_map_gradient: bfloat16 [8, 64, 8, 8, 1024], P('pipe', 'tensor')
Inputs may be any that keep to these rules, and one draw needn't show every extreme that they name: The first live_segment_table segments of a microbatch are live; some microbatch has all 4 live.
All inputs are finite; a program needn't handle non-finite values.
Results may differ from a plain program's by a relative error of at most 0.0049.
Values may be sent and summed in bfloat16 or wider, within the bound.
A program may use at most 64 MiB of HBM per device.

v0:
```python
import jax
import jax.numpy as jnp
from jax import lax
from jax.sharding import PartitionSpec as P

SEG = 128


def partner(value, axis, apart):
    mask = 2**apart
    pairs = [(source, source ^ mask) for source in range(lax.axis_size(axis))]
    return lax.ppermute(value, axis, pairs)


def shifted(block, axis, distance):
    devices = range(lax.axis_size(axis))
    route = [((i - distance) % len(devices), i) for i in devices]
    return lax.ppermute(block, axis, route)


def choose_segment_rows(class_indicator, segment_lookup):
    return jnp.einsum(
        "pzw,wlq->pzlq", class_indicator, segment_lookup, preferred_element_type=jnp.float32
    ).astype(jnp.bfloat16)


def shards(
    output_gradient,
    forward_input,
    saved_rank_outputs,
    projection_weight,
    adapter_down_maps,
    adapter_up_maps,
    segment_adapter_class,
    live_segment_table,
):
    grad_tile = output_gradient[0, 0]
    micro_count, tile_rows, tile_cols = grad_tile.shape
    weight = projection_weight[0, 0]
    up_matrix_tile = adapter_up_maps[0, 0]
    rank_part = up_matrix_tile.shape[1]
    rank_extent = adapter_down_maps.shape[2]
    local_portion = adapter_down_maps.shape[3]
    group_size = lax.axis_size("tensor")
    total_bits = group_size.bit_length() - 1
    low_size = min(group_size, 8)
    low_bits = low_size.bit_length() - 1
    high_size = group_size // low_size
    position = lax.axis_index("tensor")
    high_index = position // low_size
    batch_rows = tile_rows * high_size
    seg_count = batch_rows // SEG
    row_ids = high_index * tile_rows + jnp.arange(tile_rows, dtype=jnp.int32)
    live_count = live_segment_table[0]
    keep_rows = (row_ids // SEG)[None, :] < live_count[:, None]
    masked_tile = jnp.where(keep_rows[:, :, None], grad_tile, jnp.zeros_like(grad_tile))
    gathered = masked_tile
    for level in range(low_bits, total_bits):
        received = partner(gathered, "tensor", level)
        leading = position >> level & 1 == 0
        gathered = jnp.where(
            leading,
            jnp.concatenate([gathered, received], 1),
            jnp.concatenate([received, gathered], 1),
        )
    products = jnp.einsum("mrd,id->mri", gathered, weight, preferred_element_type=jnp.float32)
    reduced = products
    for level in reversed(range(low_bits)):
        half_cols = reduced.shape[2] // 2
        lower_half = reduced[:, :, :half_cols]
        upper_half = reduced[:, :, half_cols:]
        upper_side = position >> level & 1 == 1
        kept_half = jnp.where(upper_side, upper_half, lower_half)
        sent_half = jnp.where(upper_side, lower_half, upper_half)
        reduced = kept_half + partner(sent_half, "tensor", level)
    classes = segment_adapter_class[0]
    class_indicator = (
        classes[:, :, None] == jnp.arange(up_matrix_tile.shape[0], dtype=jnp.int32)[None, None, :]
    ).astype(jnp.bfloat16)
    selected_up_matrix = choose_segment_rows(class_indicator, up_matrix_tile)
    grad_segs = gathered.reshape(micro_count, seg_count, SEG, tile_cols)
    partial_rank = jnp.einsum(
        "mskd,msrd->mskr", grad_segs, selected_up_matrix, preferred_element_type=jnp.float32
    )
    padded_rank = jnp.zeros((micro_count, seg_count, SEG, rank_extent), jnp.float32)
    padded_rank = lax.dynamic_update_slice_in_dim(
        padded_rank, partial_rank, high_index * rank_part, 3
    )
    lowrank = lax.psum(padded_rank, "tensor").astype(jnp.bfloat16)
    selected_down_matrix = choose_segment_rows(class_indicator, adapter_down_maps[0])
    adapter = jnp.einsum(
        "mskr,msrd->mskd", lowrank, selected_down_matrix, preferred_element_type=jnp.float32
    )
    input_gradient = (reduced + adapter.reshape(micro_count, batch_rows, local_portion)).astype(
        jnp.bfloat16
    )
    grad_prev = shifted(input_gradient, "pipe", -1)
    inputs_seg = forward_input[0].reshape(micro_count, seg_count, SEG, local_portion)
    segment_down_matrix = jnp.einsum(
        "mskr,mskd->msrd", lowrank, inputs_seg, preferred_element_type=jnp.float32
    )
    hidden = lax.all_gather(saved_rank_outputs[0], "tensor", axis=1, tiled=True)
    hidden_part = lax.dynamic_slice_in_dim(hidden, high_index * rank_part, rank_part, 2)
    hidden_seg = hidden_part.reshape(micro_count, seg_count, SEG, rank_part)
    segment_up_matrix = jnp.einsum(
        "mskr,mskd->msrd", hidden_seg, grad_segs, preferred_element_type=jnp.float32
    )
    wide_class_indicator = class_indicator.astype(jnp.float32)
    down_map_gradient = jnp.einsum(
        "exk,exlq->klq", wide_class_indicator, segment_down_matrix, precision=lax.Precision.HIGHEST
    ).astype(jnp.bfloat16)
    up_map_gradient = jnp.einsum(
        "exk,exlq->klq", wide_class_indicator, segment_up_matrix, precision=lax.Precision.HIGHEST
    ).astype(jnp.bfloat16)
    return (grad_prev[None], down_map_gradient[None], up_map_gradient[None, None])


def solution(mesh):
    in_specs = (
        P("pipe", "tensor", None, None, None),
        P("pipe", None, None, "tensor"),
        P("pipe", None, "tensor", None),
        P("pipe", "tensor", None, None),
        P("pipe", None, None, "tensor"),
        P("pipe", "tensor", None, None, None),
        P("pipe", None, None),
        P("pipe", None),
    )
    out_specs = (
        P("pipe", None, None, "tensor"),
        P("pipe", None, None, "tensor"),
        P("pipe", "tensor", None, None, None),
    )
    return jax.shard_map(shards, mesh=mesh, in_specs=in_specs, out_specs=out_specs, check_vma=False)
```

profile of v0, /device:TPU:9, one launch (start us, length us, event | category | flops | bytes accessed | tf_op | source)
XLA Modules:
  0.0 877.9 jit_solution(1295151885727014478)
XLA Ops:
  0.6 0.0 copy-start
  0.7 0.9 broadcast_compare_fusion
  1.5 1.0 bitcast_select_fusion
  2.6 3.1 collective-permute-start
  5.7 6.0 collective-permute-done
  11.7 0.1 maximum_select_fusion.2
  11.8 0.0 copy-start.6
  11.8 4.7 collective-permute-start.1
  16.5 10.8 %collective-permute-done.1 = bf16[2,128,1024]{2,1,0:T(8,128)(2,1)} collective-permute-done((bf16[2,128,1024]{2,1,0:T(8,128)(2,1)S(1)}, bf16[2,128,1024]{2,1,0:T(8,128)(2,1)}, u32[]{:S(2)}, u32[]{:S(2)}) %collective-permute-start.1) | collective-permute-done | bytes 524320 | tf_op jit(solution)/shard_map/ppermute | solution.py:12
  27.3 2.1 maximum_select_fusion.1
  29.4 6.6 collective-permute-start.2
  35.9 43.0 %collective-permute-done.2 = bf16[2,256,1024]{2,1,0:T(8,128)(2,1)} collective-permute-done((bf16[2,256,1024]{2,1,0:T(8,128)(2,1)S(1)}, bf16[2,256,1024]{2,1,0:T(8,128)(2,1)}, u32[]{:S(2)}, u32[]{:S(2)}) %collective-permute-start.2) | collective-permute-done | bytes 1048608 | tf_op jit(solution)/shard_map/ppermute | solution.py:12
  78.9 2.6 maximum_select_fusion
  81.5 2.4 fusion
  83.9 0.0 copy-start.12
  83.9 2.2 slice_select_fusion
  86.1 0.5 copy-done.5
  86.7 10.6 %collective-permute-start.3 = (f32[2,512,512]{2,1,0:T(8,128)}, f32[2,512,512]{2,1,0:T(8,128)}, u32[]{:S(2)}, u32[]{:S(2)}) collective-permute-start(f32[2,512,512]{2,1,0:T(8,128)} %slice_select_fusion), channel_id=1, source_target_pairs={{0,4},{1,5},{2,6},{3,7},{4,0},{5,1},{6,2},{7,3},{8,12},{9,13},{10,... | collective-permute-start | bytes 6291464 | tf_op jit(solution)/shard_map/ppermute | solution.py:12
  97.3 272.6 %all-gather = bf16[1,2,512,64]{3,2,1,0:T(8,128)(2,1)S(1)} all-gather(bf16[1,2,8,64]{3,2,1,0:T(8,128)(2,1)S(1)} %copy-done.12), channel_id=2, replica_groups=mesh['pipe'=8,'tensor'=64] {'tensor'}, dimensions={2}, use_global_device_ids=true | all-gather | bytes 133120 | tf_op jit(solution)/shard_map/all_gather | solution.py:102
  370.0 0.0 collective-permute-done.3
  370.0 3.6 select_add_fusion
  373.6 0.0 copy-start.3
  373.6 1.3 copy-done.3
  374.9 0.1 slice_select_fusion.1
  375.1 1.9 collective-permute-start.4
  377.0 0.1 constant_dynamic-slice_fusion
  377.2 0.9 fusion.10
  378.1 1.1 fusion.12
  379.3 2.4 convolution_dynamic-update-slice_fusion
  381.6 0.7 copy-done.7
  382.4 0.4 fusion.27
  382.8 14.4 %collective-permute-done.4 = f32[2,512,256]{2,1,0:T(8,128)} collective-permute-done((f32[2,512,256]{2,1,0:T(8,128)S(1)}, f32[2,512,256]{2,1,0:T(8,128)}, u32[]{:S(2)}, u32[]{:S(2)}) %collective-permute-start.4) | collective-permute-done | bytes 1048608 | tf_op jit(solution)/shard_map/ppermute | solution.py:12
  397.2 1.4 select_add_fusion.1
  398.6 0.0 copy-start.8
  398.6 0.8 slice_select_fusion.2
  399.4 1.9 collective-permute-start.5
  401.4 0.6 fusion.4
  401.9 0.7 copy.12
  402.7 374.2 %all-reduce.1 = bf16[2,4,128,64]{2,3,1,0:T(8,128)(2,1)S(1)} all-reduce(f32[2,4,128,64]{2,3,1,0:T(8,128)S(1)} %copy-done.8), channel_id=1, replica_groups=mesh['pipe'=8,'tensor'=64] {'tensor'}, use_global_device_ids=true, to_apply=%region_0.1 | all-reduce | flops 65536 | bytes 393216 | tf_op jit(solution)/shard_map/psum | solution.py:89
  776.9 1.2 fusion.9
  778.1 0.0 collective-permute-done.5
  778.1 1.2 fusion.6
  779.3 90.0 %collective-permute-start.6 = (bf16[2,512,128]{2,1,0:T(8,128)(2,1)S(1)}, bf16[2,512,128]{2,1,0:T(8,128)(2,1)S(1)}, u32[]{:S(2)}, u32[]{:S(2)}) collective-permute-start(bf16[2,512,128]{2,1,0:T(8,128)(2,1)S(1)} %fusion.6), channel_id=1, source_target_pairs={{64,0},{128,64},{192,128},{256,192},{320,256},{384,320},{448,384},... | collective-permute-start | bytes 786440 | tf_op jit(solution)/shard_map/ppermute | solution.py:18
  869.3 0.2 fusion.28
  869.5 0.6 fusion.5
  870.1 0.7 copy.11
  870.8 6.4 collective-permute-done.6
  877.2 0.7 copy.38
  (20 shorter events, 0.1 us)
Async XLA Ops:
  0.6 80.9 %copy-start = (bf16[1,1,1024,1024]{3,2,1,0:T(8,128)(2,1)S(1)}, bf16[1,1,1024,1024]{3,2,1,0:T(8,128)(2,1)}, u32[]{:S(2)}) copy-start(bf16[1,1,1024,1024]{3,2,1,0:T(8,128)(2,1)} %param.11) | copy-start | bytes 6291460
  2.6 9.1 %collective-permute-start = (bf16[2,64,1024]{2,1,0:T(8,128)(2,1)S(1)}, bf16[2,64,1024]{2,1,0:T(8,128)(2,1)S(1)}, u32[]{:S(2)}, u32[]{:S(2)}) collective-permute-start(bf16[2,64,1024]{2,1,0:T(8,128)(2,1)S(1)} %bitcast_select_fusion), channel_id=1, source_target_pairs={{0,8},{1,9},{2,10},{3,11},{4,12},{5,13},{6,14},{7,15},{8,0},{9,1},... | collective-permute-start | bytes 786440 | tf_op jit(solution)/shard_map/ppermute | solution.py:12
  11.8 4.7 copy-start.6
  11.8 15.5 %collective-permute-start.1 = (bf16[2,128,1024]{2,1,0:T(8,128)(2,1)S(1)}, bf16[2,128,1024]{2,1,0:T(8,128)(2,1)}, u32[]{:S(2)}, u32[]{:S(2)}) collective-permute-start(bf16[2,128,1024]{2,1,0:T(8,128)(2,1)S(1)} %maximum_select_fusion.2), channel_id=1, source_target_pairs={{0,16},{1,17},{2,18},{3,19},{4,20},{5,21},{6,22},{7,23},{8,24},{9,... | collective-permute-start | bytes 1572872 | tf_op jit(solution)/shard_map/ppermute | solution.py:12
  29.4 49.6 %collective-permute-start.2 = (bf16[2,256,1024]{2,1,0:T(8,128)(2,1)S(1)}, bf16[2,256,1024]{2,1,0:T(8,128)(2,1)}, u32[]{:S(2)}, u32[]{:S(2)}) collective-permute-start(bf16[2,256,1024]{2,1,0:T(8,128)(2,1)S(1)} %maximum_select_fusion.1), channel_id=1, source_target_pairs={{0,32},{1,33},{2,34},{3,35},{4,36},{5,37},{6,38},{7,39},{8,40},{9,... | collective-permute-start | bytes 3145736 | tf_op jit(solution)/shard_map/ppermute | solution.py:12
  81.5 2.4 copy-start.1
  83.9 2.7 copy-start.5
  83.9 13.4 %copy-start.12 = (bf16[1,2,8,64]{3,2,1,0:T(8,128)(2,1)S(1)}, bf16[1,2,8,64]{3,2,1,0:T(8,128)(2,1)}, u32[]{:S(2)}) copy-start(bf16[1,2,8,64]{3,2,1,0:T(8,128)(2,1)} %param.10) | copy-start | bytes 6148
  86.7 283.3 %collective-permute-start.3 = (f32[2,512,512]{2,1,0:T(8,128)}, f32[2,512,512]{2,1,0:T(8,128)}, u32[]{:S(2)}, u32[]{:S(2)}) collective-permute-start(f32[2,512,512]{2,1,0:T(8,128)} %slice_select_fusion), channel_id=1, source_target_pairs={{0,4},{1,5},{2,6},{3,7},{4,0},{5,1},{6,2},{7,3},{8,12},{9,13},{10,... | collective-permute-start | bytes 6291464 | tf_op jit(solution)/shard_map/ppermute | solution.py:12
  373.6 1.3 copy-start.3
  374.9 2.2 copy-start.10
  374.9 2.2 copy-start.11
  375.1 22.1 %collective-permute-start.4 = (f32[2,512,256]{2,1,0:T(8,128)S(1)}, f32[2,512,256]{2,1,0:T(8,128)}, u32[]{:S(2)}, u32[]{:S(2)}) collective-permute-start(f32[2,512,256]{2,1,0:T(8,128)S(1)} %slice_select_fusion.1), channel_id=1, source_target_pairs={{0,2},{1,3},{2,0},{3,1},{4,6},{5,7},{6,4},{7,5},{8,10},{9,11},{10,... | collective-permute-start | bytes 3145736 | tf_op jit(solution)/shard_map/ppermute | solution.py:12
  377.1 5.2 copy-start.2
  379.2 17.9 %copy-start.4 = (f32[2,512,512]{2,1,0:T(8,128)S(1)}, f32[2,512,512]{2,1,0:T(8,128)}, u32[]{:S(2)}) copy-start(f32[2,512,512]{2,1,0:T(8,128)} %copy-done.3) | copy-start | bytes 6291460
  381.6 0.7 copy-start.7
  398.6 4.1 copy-start.8
  399.4 378.6 %collective-permute-start.5 = (f32[2,512,128]{2,1,0:T(8,128)}, f32[2,512,128]{2,1,0:T(8,128)}, u32[]{:S(2)}, u32[]{:S(2)}) collective-permute-start(f32[2,512,128]{2,1,0:T(8,128)} %slice_select_fusion.2), channel_id=1, source_target_pairs={{0,1},{1,0},{2,3},{3,2},{4,5},{5,4},{6,7},{7,6},{8,9},{9,8},{10,11... | collective-permute-start | bytes 1572872 | tf_op jit(solution)/shard_map/ppermute | solution.py:12
  776.9 92.5 %copy-start.9 = (bf16[1,2,512,128]{3,2,1,0:T(8,128)(2,1)S(1)}, bf16[1,2,512,128]{3,2,1,0:T(8,128)(2,1)}, u32[]{:S(2)}) copy-start(bf16[1,2,512,128]{3,2,1,0:T(8,128)(2,1)} %param.9) | copy-start | bytes 786436
  779.3 97.9 %collective-permute-start.6 = (bf16[2,512,128]{2,1,0:T(8,128)(2,1)S(1)}, bf16[2,512,128]{2,1,0:T(8,128)(2,1)S(1)}, u32[]{:S(2)}, u32[]{:S(2)}) collective-permute-start(bf16[2,512,128]{2,1,0:T(8,128)(2,1)S(1)} %fusion.6), channel_id=1, source_target_pairs={{64,0},{128,64},{192,128},{256,192},{320,256},{384,320},{448,384},... | collective-permute-start | bytes 786440 | tf_op jit(solution)/shard_map/ppermute | solution.py:18
where the time goes:
time: 878 us
  blocking collectives  647 us (74%)
  starting transfers between devices  119 us (14%)
  waiting for transfers between devices  80.5 us (9%)
  other arithmetic  16.1 us (2%)
  matrix products  9.77 us (1%)
    psum x1, blocking collectives, shards(): lowrank = lax.psum(padded_rank, 'tensor').astype(jnp.bfloat16)  374 us
    all_gather x1, blocking collectives, shards(): hidden = lax.all_gather(saved_rank_outputs[0], 'tensor', axis=1, tiled=True)  273 us
    ppermute x1, starting transfers between devices, shifted(): return lax.ppermute(block, axis, route)  90 us
    ppermute x6, waiting for transfers between devices, partner(): return lax.ppermute(value, axis, pairs)  74.1 us
    ppermute x6, starting transfers between devices, partner(): return lax.ppermute(value, axis, pairs)  28.8 us
  transfers between devices with their start and end apart: 7, of which 5 were waited for; matrix products, arithmetic and copies ran while one was open for 1% of the time, Pallas kernels for 0%

commit v1 on v0

--- a/solution.py
+++ b/solution.py
@@ -4,6 +4,12 @@
 from jax.sharding import PartitionSpec as P
 
 SEG = 128
+
+
+def gather_and_add(shard, mesh_axis):
+    parts = lax.all_gather(shard, mesh_axis, axis=0, tiled=False)
+    total = parts.sum(axis=0)
+    return total
 
 
 def partner(value, axis, apart):
@@ -86,7 +92,7 @@
     padded_rank = lax.dynamic_update_slice_in_dim(
         padded_rank, partial_rank, high_index * rank_part, 3
     )
-    lowrank = lax.psum(padded_rank, "tensor").astype(jnp.bfloat16)
+    lowrank = gather_and_add(padded_rank, "tensor").astype(jnp.bfloat16)
     selected_down_matrix = choose_segment_rows(class_indicator, adapter_down_maps[0])
     adapter = jnp.einsum(
         "mskr,msrd->mskd", lowrank, selected_down_matrix, preferred_element_type=jnp.float32

time: 878 us -> 535 us (0.61)
  blocking collectives: 647 us -> 259 us
  waiting for transfers between devices: 80.5 us -> 122 us
  starting transfers between devices: 119 us -> 102 us
  between operations: 0.98 us -> 14.4 us
    psum x1 -> x0, blocking collectives: 374 us -> none  [shards(): lowrank = lax.psum(padded_rank, 'tensor').astype(jnp.bfloat16)]
    ppermute x1, starting transfers between devices: 90 us -> 23.9 us  [shifted(): return lax.ppermute(block, axis, route)]
    ppermute x6, starting transfers between devices: 28.8 us -> 78 us  [partner(): return lax.ppermute(value, axis, pairs)]
    ppermute x6, waiting for transfers between devices: 74.1 us -> 110 us  [partner(): return lax.ppermute(value, axis, pairs)]
    all_gather x1, blocking collectives: 273 us -> 259 us  [shards(): hidden = lax.all_gather(saved_rank_outputs[0], 'tensor', axis=1, tiled=True)]
  transfers between devices with their start and end apart: 7 -> 8, of which waited for: 5 -> 5; matrix products, arithmetic and copies ran while one was open for 1% -> 4% of each run, Pallas kernels for 0% -> 0%
where the time goes in v1:
time: 535 us; the launch traced here: 534 us
  blocking collectives  259 us (48%)
  waiting for transfers between devices  122 us (23%)
  starting transfers between devices  102 us (19%)
  other arithmetic  23.8 us (4%)
  between operations  14.4 us (3%)
  matrix products  7.11 us (1%)
  local copies, waits for them, and re-layouts  6.23 us (1%)
    all_gather x1, blocking collectives, shards(): hidden = lax.all_gather(saved_rank_outputs[0], 'tensor', axis=1, tiled=True)  259 us
    ppermute x6, waiting for transfers between devices, partner(): return lax.ppermute(value, axis, pairs)  110 us
    ppermute x6, starting transfers between devices, partner(): return lax.ppermute(value, axis, pairs)  78 us
    ppermute x1, starting transfers between devices, shifted(): return lax.ppermute(block, axis, route)  23.9 us
    ppermute x1, waiting for transfers between devices, shifted(): return lax.ppermute(block, axis, route)  11.5 us
  transfers between devices with their start and end apart: 8, of which 5 were waited for; matrix products, arithmetic and copies ran while one was open for 4% of the time, Pallas kernels for 0%

profile of v1, /device:TPU:9, one launch (start us, length us, event | category | flops | bytes accessed | tf_op | source)
XLA Modules:
  0.0 534.2 jit_solution(14032122340949293294)
XLA Ops:
  7.2 0.0 copy-start
  7.2 0.0 all-gather.3.cloned.1.call-start
  7.3 0.9 broadcast_compare_fusion
  8.1 1.0 bitcast_select_fusion
  9.2 3.1 collective-permute-start
  12.3 6.0 %collective-permute-done = bf16[2,64,1024]{2,1,0:T(8,128)(2,1)S(1)} collective-permute-done((bf16[2,64,1024]{2,1,0:T(8,128)(2,1)S(1)}, bf16[2,64,1024]{2,1,0:T(8,128)(2,1)S(1)}, u32[]{:S(2)}, u32[]{:S(2)}) %collective-permute-start) | collective-permute-done | bytes 262176 | tf_op jit(solution)/shard_map/ppermute | solution.py:18
  18.3 0.1 maximum_select_fusion.2
  18.4 4.7 collective-permute-start.1
  23.1 10.8 %collective-permute-done.1 = bf16[2,128,1024]{2,1,0:T(8,128)(2,1)} collective-permute-done((bf16[2,128,1024]{2,1,0:T(8,128)(2,1)S(1)}, bf16[2,128,1024]{2,1,0:T(8,128)(2,1)}, u32[]{:S(2)}, u32[]{:S(2)}) %collective-permute-start.1) | collective-permute-done | bytes 524320 | tf_op jit(solution)/shard_map/ppermute | solution.py:18
  33.9 2.0 maximum_select_fusion.1
  35.9 6.6 %collective-permute-start.2 = (bf16[2,256,1024]{2,1,0:T(8,128)(2,1)S(1)}, bf16[2,256,1024]{2,1,0:T(8,128)(2,1)}, u32[]{:S(2)}, u32[]{:S(2)}) collective-permute-start(bf16[2,256,1024]{2,1,0:T(8,128)(2,1)S(1)} %maximum_select_fusion.1), channel_id=1, source_target_pairs={{0,32},{1,33},{2,34},{3,35},{4,36},{5,37},{6,38},{7,39},{8,40},{9,... | collective-permute-start | bytes 3145736 | tf_op jit(solution)/shard_map/ppermute | solution.py:18
  42.5 0.2 fusion.13
  42.7 42.7 %collective-permute-done.2 = bf16[2,256,1024]{2,1,0:T(8,128)(2,1)} collective-permute-done((bf16[2,256,1024]{2,1,0:T(8,128)(2,1)S(1)}, bf16[2,256,1024]{2,1,0:T(8,128)(2,1)}, u32[]{:S(2)}, u32[]{:S(2)}) %collective-permute-start.2) | collective-permute-done | bytes 1048608 | tf_op jit(solution)/shard_map/ppermute | solution.py:18
  85.4 2.5 maximum_select_fusion
  88.0 1.3 copy-done.1
  89.3 0.6 fusion.6
  90.0 0.7 copy-done.6
  90.7 0.0 all-gather.3.cloned.1.call-update
  90.7 4.0 fusion
  94.7 2.2 slice_select_fusion
  96.9 0.5 copy-done.4
  97.5 10.6 %collective-permute-start.3 = (f32[2,512,512]{2,1,0:T(8,128)}, f32[2,512,512]{2,1,0:T(8,128)}, u32[]{:S(2)}, u32[]{:S(2)}) collective-permute-start(f32[2,512,512]{2,1,0:T(8,128)} %slice_select_fusion), channel_id=1, source_target_pairs={{0,4},{1,5},{2,6},{3,7},{4,0},{5,1},{6,2},{7,3},{8,12},{9,13},{10,... | collective-permute-start | bytes 6291464 | tf_op jit(solution)/shard_map/ppermute | solution.py:18
  108.1 50.7 %collective-permute-done.3 = f32[2,512,512]{2,1,0:T(8,128)} collective-permute-done((f32[2,512,512]{2,1,0:T(8,128)}, f32[2,512,512]{2,1,0:T(8,128)}, u32[]{:S(2)}, u32[]{:S(2)}) %collective-permute-start.3) | collective-permute-done | bytes 2097184 | tf_op jit(solution)/shard_map/ppermute | solution.py:18
  158.8 3.6 select_add_fusion
  162.5 1.3 copy-done.3
  163.8 0.1 slice_select_fusion.1
  163.9 51.1 %collective-permute-start.4 = (f32[2,512,256]{2,1,0:T(8,128)S(1)}, f32[2,512,256]{2,1,0:T(8,128)}, u32[]{:S(2)}, u32[]{:S(2)}) collective-permute-start(f32[2,512,256]{2,1,0:T(8,128)S(1)} %slice_select_fusion.1), channel_id=1, source_target_pairs={{0,2},{1,3},{2,0},{3,1},{4,6},{5,7},{6,4},{7,5},{8,10},{9,11},{10,... | collective-permute-start | bytes 3145736 | tf_op jit(solution)/shard_map/ppermute | solution.py:18
  215.1 259.1 %all-gather = bf16[1,2,512,64]{3,2,1,0:T(8,128)(2,1)S(1)} all-gather(bf16[1,2,8,64]{3,2,1,0:T(8,128)(2,1)S(1)} %copy-done.11), channel_id=2, replica_groups=mesh['pipe'=8,'tensor'=64] {'tensor'}, dimensions={2}, use_global_device_ids=true | all-gather | bytes 133120 | tf_op jit(solution)/shard_map/all_gather | solution.py:108
  474.1 0.1 constant_dynamic-slice_fusion
  474.3 0.2 fusion.11
  474.5 0.0 collective-permute-done.4
  474.6 2.2 select_add_fusion.1
  476.8 0.9 slice_select_fusion.2
  477.6 1.9 collective-permute-start.5
  479.6 0.4 fusion.28
  480.0 0.6 fusion.4
  480.5 0.7 copy.14
  481.3 7.0 %reduce_sum.9 = bf16[2,4,128,64]{2,3,1,0:T(8,128)(2,1)S(1)} reduce(f32[64,2,4,128,64]{3,4,2,1,0:T(8,128)} %all-gather.3.cloned.1.call-done, f32[]{:T(128)} %constant.48.clone.1), dimensions={0}, to_apply=%region_0.1 | reduce | flops 4128768 | bytes 16908292 | tf_op jit(solution)/shard_map/reduce_sum | solution.py:11
  488.3 0.0 copy-start.7
  488.3 0.3 fusion.10
  488.6 0.0 collective-permute-done.5
  488.6 1.2 fusion.7
  489.8 23.9 %collective-permute-start.6 = (bf16[2,512,128]{2,1,0:T(8,128)(2,1)S(1)}, bf16[2,512,128]{2,1,0:T(8,128)(2,1)S(1)}, u32[]{:S(2)}, u32[]{:S(2)}) collective-permute-start(bf16[2,512,128]{2,1,0:T(8,128)(2,1)S(1)} %fusion.7), channel_id=1, source_target_pairs={{64,0},{128,64},{192,128},{256,192},{320,256},{384,320},{448,384},... | collective-permute-start | bytes 786440 | tf_op jit(solution)/shard_map/ppermute | solution.py:24
  513.7 0.2 fusion.29
  513.9 0.6 fusion.5
  514.4 0.7 copy.13
  515.1 11.5 %collective-permute-done.6 = bf16[2,512,128]{2,1,0:T(8,128)(2,1)S(1)} collective-permute-done((bf16[2,512,128]{2,1,0:T(8,128)(2,1)S(1)}, bf16[2,512,128]{2,1,0:T(8,128)(2,1)S(1)}, u32[]{:S(2)}, u32[]{:S(2)}) %collective-permute-start.6) | collective-permute-done | bytes 262176 | tf_op jit(solution)/shard_map/ppermute | solution.py:24
  526.6 0.7 copy.38
  (21 shorter events, 0.1 us)
Async XLA Ops:
  7.2 83.6 %copy-start = (bf16[1,1,1024,1024]{3,2,1,0:T(8,128)(2,1)S(1)}, bf16[1,1,1024,1024]{3,2,1,0:T(8,128)(2,1)}, u32[]{:S(2)}) copy-start(bf16[1,1,1024,1024]{3,2,1,0:T(8,128)(2,1)} %param.11) | copy-start | bytes 6291460
  7.2 35.3 %copy-start.10 = (s32[1,2,4]{2,1,0:T(2,128)S(1)}, s32[1,2,4]{2,1,0:T(2,128)}, u32[]{:S(2)}) copy-start(s32[1,2,4]{2,1,0:T(2,128)} %param.14) | copy-start | bytes 100
  7.2 35.3 %copy-start.8 = (bf16[1,1,8,8,1024]{4,3,2,1,0:T(8,128)(2,1)S(1)}, bf16[1,1,8,8,1024]{4,3,2,1,0:T(8,128)(2,1)}, u32[]{:S(2)}) copy-start(bf16[1,1,8,8,1024]{4,3,2,1,0:T(8,128)(2,1)} %param.13) | copy-start | bytes 393220
  7.2 474.1 %all-gather.3.cloned.1.call-start = ((), (), s32[]{:S(2)}) async-start(), calls=%async_computation | async-start | bytes 17039360 | tf_op jit(solution)/shard_map/all_gather | solution.py:10
  9.2 9.1 %collective-permute-start = (bf16[2,64,1024]{2,1,0:T(8,128)(2,1)S(1)}, bf16[2,64,1024]{2,1,0:T(8,128)(2,1)S(1)}, u32[]{:S(2)}, u32[]{:S(2)}) collective-permute-start(bf16[2,64,1024]{2,1,0:T(8,128)(2,1)S(1)} %bitcast_select_fusion), channel_id=1, source_target_pairs={{0,8},{1,9},{2,10},{3,11},{4,12},{5,13},{6,14},{7,15},{8,0},{9,1},... | collective-permute-start | bytes 786440 | tf_op jit(solution)/shard_map/ppermute | solution.py:18
  18.4 4.7 copy-start.5
  18.4 15.5 %collective-permute-start.1 = (bf16[2,128,1024]{2,1,0:T(8,128)(2,1)S(1)}, bf16[2,128,1024]{2,1,0:T(8,128)(2,1)}, u32[]{:S(2)}, u32[]{:S(2)}) collective-permute-start(bf16[2,128,1024]{2,1,0:T(8,128)(2,1)S(1)} %maximum_select_fusion.2), channel_id=1, source_target_pairs={{0,16},{1,17},{2,18},{3,19},{4,20},{5,21},{6,22},{7,23},{8,24},{9,... | collective-permute-start | bytes 1572872 | tf_op jit(solution)/shard_map/ppermute | solution.py:18
  35.9 49.6 %collective-permute-start.2 = (bf16[2,256,1024]{2,1,0:T(8,128)(2,1)S(1)}, bf16[2,256,1024]{2,1,0:T(8,128)(2,1)}, u32[]{:S(2)}, u32[]{:S(2)}) collective-permute-start(bf16[2,256,1024]{2,1,0:T(8,128)(2,1)S(1)} %maximum_select_fusion.1), channel_id=1, source_target_pairs={{0,32},{1,33},{2,34},{3,35},{4,36},{5,37},{6,38},{7,39},{8,40},{9,... | collective-permute-start | bytes 3145736 | tf_op jit(solution)/shard_map/ppermute | solution.py:18
  88.0 1.4 copy-start.1
  90.0 0.7 copy-start.6
  94.7 2.7 copy-start.4
  97.5 61.4 %collective-permute-start.3 = (f32[2,512,512]{2,1,0:T(8,128)}, f32[2,512,512]{2,1,0:T(8,128)}, u32[]{:S(2)}, u32[]{:S(2)}) collective-permute-start(f32[2,512,512]{2,1,0:T(8,128)} %slice_select_fusion), channel_id=1, source_target_pairs={{0,4},{1,5},{2,6},{3,7},{4,0},{5,1},{6,2},{7,3},{8,12},{9,13},{10,... | collective-permute-start | bytes 6291464 | tf_op jit(solution)/shard_map/ppermute | solution.py:18
  162.5 1.3 copy-start.3
  163.8 51.3 %copy-start.11 = (bf16[1,2,8,64]{3,2,1,0:T(8,128)(2,1)S(1)}, bf16[1,2,8,64]{3,2,1,0:T(8,128)(2,1)}, u32[]{:S(2)}) copy-start(bf16[1,2,8,64]{3,2,1,0:T(8,128)(2,1)} %param.10) | copy-start | bytes 6148
  163.8 310.5 %copy-start.9 = (bf16[1,8,64,128]{3,2,1,0:T(8,128)(2,1)S(1)}, bf16[1,8,64,128]{3,2,1,0:T(8,128)(2,1)}, u32[]{:S(2)}) copy-start(bf16[1,8,64,128]{3,2,1,0:T(8,128)(2,1)} %param.12) | copy-start | bytes 393220
  163.9 310.6 %collective-permute-start.4 = (f32[2,512,256]{2,1,0:T(8,128)S(1)}, f32[2,512,256]{2,1,0:T(8,128)}, u32[]{:S(2)}, u32[]{:S(2)}) collective-permute-start(f32[2,512,256]{2,1,0:T(8,128)S(1)} %slice_select_fusion.1), channel_id=1, source_target_pairs={{0,2},{1,3},{2,0},{3,1},{4,6},{5,7},{6,4},{7,5},{8,10},{9,11},{10,... | collective-permute-start | bytes 3145736 | tf_op jit(solution)/shard_map/ppermute | solution.py:18
  474.5 5.0 copy-start.2
  477.6 11.0 %collective-permute-start.5 = (f32[2,512,128]{2,1,0:T(8,128)}, f32[2,512,128]{2,1,0:T(8,128)}, u32[]{:S(2)}, u32[]{:S(2)}) collective-permute-start(f32[2,512,128]{2,1,0:T(8,128)} %slice_select_fusion.2), channel_id=1, source_target_pairs={{0,1},{1,0},{2,3},{3,2},{4,5},{5,4},{6,7},{7,6},{8,9},{9,8},{10,11... | collective-permute-start | bytes 1572872 | tf_op jit(solution)/shard_map/ppermute | solution.py:18
  488.3 25.4 %copy-start.7 = (bf16[1,2,512,128]{3,2,1,0:T(8,128)(2,1)S(1)}, bf16[1,2,512,128]{3,2,1,0:T(8,128)(2,1)}, u32[]{:S(2)}) copy-start(bf16[1,2,512,128]{3,2,1,0:T(8,128)(2,1)} %param.9) | copy-start | bytes 786436
  489.8 36.9 %collective-permute-start.6 = (bf16[2,512,128]{2,1,0:T(8,128)(2,1)S(1)}, bf16[2,512,128]{2,1,0:T(8,128)(2,1)S(1)}, u32[]{:S(2)}, u32[]{:S(2)}) collective-permute-start(bf16[2,512,128]{2,1,0:T(8,128)(2,1)S(1)} %fusion.7), channel_id=1, source_target_pairs={{64,0},{128,64},{192,128},{256,192},{320,256},{384,320},{448,384},... | collective-permute-start | bytes 786440 | tf_op jit(solution)/shard_map/ppermute | solution.py:24
Sparse Core Ops, SparseCore 0:
  90.9 359.4 all-gather.2
